TPU v7x, 32 devices: a whole 2x2x4 slice. The times are simulated.
32 devices in a mesh: row: 8 (over y, x, core), col: 4 (over z).
Axes of the slice: x: 2, y: 2, z: 4, core: 2. Of those that a mesh axis runs over, the one named last changes fastest.
Arguments:
- earlier_blocks: bfloat16 [32, 8, 128, 128], P('row', 'col'), may hold values from -0.5 to 0.5
- later_blocks: bfloat16 [8, 32, 128, 128], P('row', 'col'), may hold values from -6 to 6
- earlier_pattern: int32 [32, 8], P('row', 'col'), may hold values from 0 to 1, as said below
- later_pattern: int32 [8, 32], P('row', 'col'), may hold values from 0 to 1, as said below
- triples: int32 [32, 32, 48], P('row', 'col'), may hold values from 0 to 7
Outputs:
- composed: float32 [32, 32, 128, 128], P('row', 'col')
Inputs may be any that keep to these rules, and one draw needn't show every extreme that they name: `earlier_pattern`: in each aligned share of 4 x 2 entries held by one device, at most 4 entries are 1, and exactly 4 in some share. `later_pattern`: in each aligned share of 1 x 8 entries held by one device, at most 4 entries are 1, and exactly 4 in some share.
All inputs are finite; a program needn't handle non-finite values.
Results may differ from a plain program's by a relative error of at most 0.0003.
Values may be sent and summed in bfloat16 or wider, within the bound.
A program may use at most 256 MiB of HBM per device.

v0:
```python
import jax
import jax.numpy as jnp
from jax import lax
from jax.sharding import PartitionSpec as P


def compose_blocks(earlier_full, later_full, triples):
    count_rows = triples.shape[0]
    middle = earlier_full.shape[1]
    middle_numbers = jnp.arange(middle, dtype=jnp.int32)
    counts = jnp.sum(
        (triples[:, :, :, None] == middle_numbers[None, None, None, :]).astype(jnp.float32), axis=2
    )
    results = []
    for row_number in range(count_rows):
        products = jnp.einsum(
            "kab,kjbc->kjac",
            earlier_full[row_number],
            later_full,
            preferred_element_type=jnp.float32,
        )
        results.append(
            jnp.einsum(
                "jk,kjac->jac", counts[row_number], products, precision=lax.Precision.HIGHEST
            )
        )
    return jnp.stack(results, axis=0)


def on_device(earlier_blocks, later_blocks, earlier_pattern, later_pattern, triples):
    masked_early = earlier_blocks * earlier_pattern[:, :, None, None].astype(earlier_blocks.dtype)
    earlier_full = lax.all_gather(masked_early, "col", axis=1, tiled=True)
    masked_late = later_blocks * later_pattern[:, :, None, None].astype(later_blocks.dtype)
    later_full = lax.all_gather(masked_late, "row", axis=0, tiled=True)
    return compose_blocks(earlier_full, later_full, triples)


def solution(mesh):
    return jax.shard_map(
        on_device,
        mesh=mesh,
        in_specs=(
            P("row", "col", None, None),
            P("row", "col", None, None),
            P("row", "col"),
            P("row", "col"),
            P("row", "col", None),
        ),
        out_specs=P("row", "col", None, None),
        check_vma=False,
    )
```

profile of v0, /device:TPU:0, one launch (start us, length us, event | category | flops | bytes accessed | tf_op | source)
XLA Modules:
  0.0 129.0 jit_solution(241129378847575528)
XLA Ops:
  6.5 0.7 convert_element_type.21
  7.2 0.1 copy.8
  7.3 1.7 %broadcast_multiply_fusion = bf16[4,2,128,128]{3,2,1,0:T(8,128)(2,1)} fusion(bf16[4,2,128,128]{3,2,1,0:T(8,128)(2,1)} %param.5, bf16[4,2]{1,0:T(4,128)(2,1)S(1)} %copy.8), kind=kLoop, calls=%fused_computation.9 | loop fusion | flops 131072 | bytes 524304 | tf_op jit(solution)/shard_map/mul | solution.py:31
  9.1 0.0 all-gather.5.cloned.1.call-update
  9.1 0.0 all-gather.3.cloned.1.call-start
  9.1 0.7 convert_bitcast_fusion
  9.8 1.7 %broadcast_multiply_fusion.1 = bf16[1,8,128,128]{3,2,1,0:T(8,128)(2,1)} fusion(bf16[1,8,128,128]{3,2,1,0:T(8,128)(2,1)} %param.6, bf16[8]{0:T(256)(128)(2,1)S(1)} %convert_bitcast_fusion), kind=kLoop, calls=%fused_computation.10 | loop fusion | flops 131072 | bytes 524304 | tf_op jit(solution)/shard_map/mul | solution.py:33
  11.5 0.0 all-gather.3.cloned.1.call-update
  11.6 0.8 convert_reduce_fusion
  12.4 27.5 %all-gather.5.cloned.1.call-done = bf16[4,8,128,128]{3,2,1,0:T(8,128)(2,1)} async-done(((bf16[4,2,128,128]{3,2,1,0:T(8,128)(2,1)}), bf16[4,8,128,128]{3,2,1,0:T(8,128)(2,1)}) %all-gather.5.cloned.1.call-update) | async-done | bytes 1048592 | tf_op jit(solution)/shard_map/all_gather | solution.py:32
  40.0 29.1 %all-gather.3.cloned.1.call-done = bf16[8,8,128,128]{3,2,1,0:T(8,128)(2,1)} async-done(((bf16[1,8,128,128]{3,2,1,0:T(8,128)(2,1)}), bf16[8,8,128,128]{3,2,1,0:T(8,128)(2,1)}) %all-gather.3.cloned.1.call-update) | async-done | bytes 2097168 | tf_op jit(solution)/shard_map/all_gather | solution.py:34
  69.0 4.4 %convolution_bitcast_fusion = f32[8,8,128,128]{2,3,1,0:T(8,128)} fusion(bf16[8,8,128,128]{3,2,1,0:T(8,128)(2,1)} %all-gather.3.cloned.1.call-done, bf16[4,8,128,128]{3,2,1,0:T(8,128)(2,1)} %all-gather.5.cloned.1.call-done), kind=kOutput, calls=%fused_computation | convolution fusion | flops 268435456 | bytes 6553600 | tf_op jit(solution)/shard_map/kab,kjbc->kjac/dot_general | solution.py:16
  73.4 5.5 %copy.31 = f32[8,8,128,128]{3,0,2,1:T(8,128)} copy(f32[8,8,128,128]{2,3,1,0:T(8,128)} %convolution_bitcast_fusion) | data formatting | bytes 8388608 | tf_op jit(solution)/shard_map/kab,kjbc->kjac/transpose | solution.py:16
  78.9 2.8 %convolution_bitcast_fusion.1 = f32[8,8,128,128]{2,3,1,0:T(8,128)} fusion(bf16[8,8,128,128]{3,2,1,0:T(8,128)(2,1)S(1)} %copy-done, bf16[4,8,128,128]{3,2,1,0:T(8,128)(2,1)S(1)} %copy-done.4), kind=kOutput, calls=%fused_computation.1 | convolution fusion | flops 268435456 | bytes 6553600 | tf_op jit(solution)/shard_map/kab,kjbc->kjac/dot_general | solution.py:16
  81.7 5.4 %copy.26 = f32[8,8,128,128]{3,0,2,1:T(8,128)} copy(f32[8,8,128,128]{2,3,1,0:T(8,128)} %convolution_bitcast_fusion.1) | data formatting | bytes 8388608 | tf_op jit(solution)/shard_map/kab,kjbc->kjac/transpose | solution.py:16
  87.1 2.7 %convolution_bitcast_fusion.2 = f32[8,8,128,128]{2,3,1,0:T(8,128)} fusion(bf16[8,8,128,128]{3,2,1,0:T(8,128)(2,1)S(1)} %copy-done, bf16[4,8,128,128]{3,2,1,0:T(8,128)(2,1)S(1)} %copy-done.4), kind=kOutput, calls=%fused_computation.2 | convolution fusion | flops 268435456 | bytes 6553600 | tf_op jit(solution)/shard_map/kab,kjbc->kjac/dot_general | solution.py:16
  89.8 5.4 %copy.21 = f32[8,8,128,128]{3,0,2,1:T(8,128)} copy(f32[8,8,128,128]{2,3,1,0:T(8,128)} %convolution_bitcast_fusion.2) | data formatting | bytes 8388608 | tf_op jit(solution)/shard_map/kab,kjbc->kjac/transpose | solution.py:16
  95.2 2.7 %convolution_bitcast_fusion.3 = f32[8,8,128,128]{2,3,1,0:T(8,128)} fusion(bf16[8,8,128,128]{3,2,1,0:T(8,128)(2,1)S(1)} %copy-done, bf16[4,8,128,128]{3,2,1,0:T(8,128)(2,1)S(1)} %copy-done.4), kind=kOutput, calls=%fused_computation.3 | convolution fusion | flops 268435456 | bytes 6553600 | tf_op jit(solution)/shard_map/kab,kjbc->kjac/dot_general | solution.py:16
  98.0 5.3 %copy.16 = f32[8,8,128,128]{3,0,2,1:T(8,128)} copy(f32[8,8,128,128]{2,3,1,0:T(8,128)} %convolution_bitcast_fusion.3) | data formatting | bytes 8388608 | tf_op jit(solution)/shard_map/kab,kjbc->kjac/transpose | solution.py:16
  103.3 6.1 %fusion.4 = f32[8,1,128,128]{3,1,2,0:T(1,128)S(1)} fusion(f32[8,8,1,1]{1,2,3,0:T(1,128)S(1)} %bitcast.85, f32[8,8,128,128]{3,0,2,1:T(8,128)} %copy.31), kind=kOutput, calls=%fused_computation.18 | convolution fusion | flops 12582912 | bytes 4718848 | tf_op jit(solution)/shard_map/jk,kjac->jac/dot_general | solution.py:23
  109.5 3.7 %fusion.3 = f32[8,1,128,128]{3,1,2,0:T(1,128)S(1)} fusion(f32[8,8,1,1]{1,2,3,0:T(1,128)S(1)} %bitcast.84, f32[8,8,128,128]{3,0,2,1:T(8,128)S(1)} %copy-done.1), kind=kOutput, calls=%fused_computation.17 | convolution fusion | flops 12582912 | bytes 4718848 | tf_op jit(solution)/shard_map/jk,kjac->jac/dot_general | solution.py:23
  113.2 3.7 %fusion.2 = f32[8,1,128,128]{3,1,2,0:T(1,128)S(1)} fusion(f32[8,8,1,1]{1,2,3,0:T(1,128)S(1)} %bitcast.83, f32[8,8,128,128]{3,0,2,1:T(8,128)S(1)} %copy-done.2), kind=kOutput, calls=%fused_computation.16 | convolution fusion | flops 12582912 | bytes 4718848 | tf_op jit(solution)/shard_map/jk,kjac->jac/dot_general | solution.py:23
  117.0 3.7 %fusion.1 = f32[8,1,128,128]{3,1,2,0:T(1,128)S(1)} fusion(f32[8,8,1,1]{1,2,3,0:T(1,128)S(1)} %bitcast.82, f32[8,8,128,128]{3,0,2,1:T(8,128)S(1)} %copy-done.3), kind=kOutput, calls=%fused_computation.15 | convolution fusion | flops 12582912 | bytes 4718848 | tf_op jit(solution)/shard_map/jk,kjac->jac/dot_general | solution.py:23
  120.7 1.5 %pad_maximum_fusion = f32[4,8,128,128]{3,2,1,0:T(8,128)} fusion(f32[1,8,128,128]{3,2,1,0:T(8,128)S(1)} %bitcast.78, f32[1,8,128,128]{3,2,1,0:T(8,128)S(1)} %bitcast.79, f32[1,8,128,128]{3,2,1,0:T(8,128)S(1)} %bitcast.80, f32[1,8,128,128]{3,2,1,0:T(8,128)S(1)} %bitcast.81), kind=kLoop, calls=%fused_computation.4 | loop fusion | flops 1572864 | bytes 4194304 | tf_op jit(solution)/shard_map/stack | solution.py:27
  (12 shorter events, 0.0 us)
Async XLA Ops:
  6.5 33.4 %all-gather.5.cloned.1.call-start = ((), (), s32[]{:S(2)}) async-start(), calls=%async_computation.1 | async-start | bytes 1310720 | tf_op jit(solution)/shard_map/all_gather | solution.py:32
  9.1 59.9 %all-gather.3.cloned.1.call-start = ((), (), s32[]{:S(2)}) async-start(), calls=%async_computation | async-start | bytes 2359296 | tf_op jit(solution)/shard_map/all_gather | solution.py:34
  73.4 5.5 %copy-start = (bf16[8,8,128,128]{3,2,1,0:T(8,128)(2,1)S(1)}, bf16[8,8,128,128]{3,2,1,0:T(8,128)(2,1)}, u32[]{:S(2)}) copy-start(bf16[8,8,128,128]{3,2,1,0:T(8,128)(2,1)} %all-gather.3.cloned.1.call-done) | copy-start | bytes 6291460
  73.4 5.5 %copy-start.4 = (bf16[4,8,128,128]{3,2,1,0:T(8,128)(2,1)S(1)}, bf16[4,8,128,128]{3,2,1,0:T(8,128)(2,1)}, u32[]{:S(2)}) copy-start(bf16[4,8,128,128]{3,2,1,0:T(8,128)(2,1)} %all-gather.5.cloned.1.call-done) | copy-start | bytes 3145732
  103.3 6.1 %copy-start.1 = (f32[8,8,128,128]{3,0,2,1:T(8,128)S(1)}, f32[8,8,128,128]{3,0,2,1:T(8,128)}, u32[]{:S(2)}) copy-start(f32[8,8,128,128]{3,0,2,1:T(8,128)} %copy.26) | copy-start | bytes 12582916
  103.3 9.9 %copy-start.2 = (f32[8,8,128,128]{3,0,2,1:T(8,128)S(1)}, f32[8,8,128,128]{3,0,2,1:T(8,128)}, u32[]{:S(2)}) copy-start(f32[8,8,128,128]{3,0,2,1:T(8,128)} %copy.21) | copy-start | bytes 12582916
  109.4 7.5 %copy-start.3 = (f32[8,8,128,128]{3,0,2,1:T(8,128)S(1)}, f32[8,8,128,128]{3,0,2,1:T(8,128)}, u32[]{:S(2)}) copy-start(f32[8,8,128,128]{3,0,2,1:T(8,128)} %copy.16) | copy-start | bytes 12582916
Sparse Core Ops, SparseCore 0:
  9.2 30.6 all-gather.4
  41.8 27.1 all-gather.2
where the time goes:
time: 129 us
  waiting for transfers between devices  56.6 us (44%)
  matrix products  30 us (23%)
  local copies, waits for them, and re-layouts  21.8 us (17%)
  between operations  13.5 us (10%)
  other arithmetic  7.1 us (6%)
    all_gather x1, waiting for transfers between devices, on_device(): later_full = lax.all_gather(masked_late, 'row', axis=0, tiled=True)  29.1 us
    all_gather x1, waiting for transfers between devices, on_device(): earlier_full = lax.all_gather(masked_early, 'col', axis=1, tiled=True)  27.5 us
    transpose x4, local copies, waits for them, and re-layouts, compose_blocks(): jnp.einsum('kab,kjbc->kjac', earlier_full[row_number], later_full, prefer...  21.6 us
    dot_general x4, matrix products, compose_blocks(): jnp.einsum('jk,kjac->jac', counts[row_number], products, precision=lax.Pr...  17.3 us
    dot_general x4, matrix products, compose_blocks(): jnp.einsum('kab,kjbc->kjac', earlier_full[row_number], later_full, prefer...  12.6 us
  transfers between devices with their start and end apart: 2, of which 2 were waited for; matrix products, arithmetic and copies ran while one was open for 3% of the time, Pallas kernels for 0%

commit v1 on v0

--- a/solution.py
+++ b/solution.py
@@ -28,10 +28,16 @@
 
 
 def on_device(earlier_blocks, later_blocks, earlier_pattern, later_pattern, triples):
+
+    def run_pools_in(mine_x):
+        return jnp.concatenate(
+            lax.all_to_all(jnp.stack([mine_x] * lax.axis_size("row")), "row", 0, 0), axis=0
+        )
+
     masked_early = earlier_blocks * earlier_pattern[:, :, None, None].astype(earlier_blocks.dtype)
     earlier_full = lax.all_gather(masked_early, "col", axis=1, tiled=True)
     masked_late = later_blocks * later_pattern[:, :, None, None].astype(later_blocks.dtype)
-    later_full = lax.all_gather(masked_late, "row", axis=0, tiled=True)
+    later_full = run_pools_in(masked_late)
     return compose_blocks(earlier_full, later_full, triples)
 
 

time: 129 us -> 107 us (0.83)
  waiting for transfers between devices: 56.6 us -> 31 us
  starting transfers between devices: 0.04 us -> 5.24 us
  other arithmetic: 7.1 us -> 4.11 us
  local copies, waits for them, and re-layouts: 21.8 us -> 23.5 us
    all_gather x1 -> x0, waiting for transfers between devices: 29.1 us -> none  [on_device(): later_full = lax.all_gather(masked_late, 'row', axis=0, tiled=True)]
    all_to_all x0 -> x1, starting transfers between devices: none -> 5.2 us  [run_pools_in(): lax.all_to_all(jnp.stack([mine_x] * lax.axis_size('row')), 'row', 0, 0)]
    all_gather x1, waiting for transfers between devices: 27.5 us -> 31 us  [on_device(): earlier_full = lax.all_gather(masked_early, 'col', axis=1, tiled=True)]
    another operation x0 -> x1, local copies, waits for them, and re-layouts: none -> 1.83 us  [run_pools_in(): jnp.stack([mine_x] * lax.axis_size('row'))]
  transfers between devices with their start and end apart: 2 -> 2, of which waited for: 2 -> 1; matrix products, arithmetic and copies ran while one was open for 3% -> 1% of each run, Pallas kernels for 0% -> 0%
where the time goes in v1:
time: 107 us
  waiting for transfers between devices  31 us (29%)
  matrix products  29.3 us (27%)
  local copies, waits for them, and re-layouts  23.5 us (22%)
  between operations  13.5 us (13%)
  starting transfers between devices  5.24 us (5%)
  other arithmetic  4.11 us (4%)
    all_gather x1, waiting for transfers between devices, on_device(): earlier_full = lax.all_gather(masked_early, 'col', axis=1, tiled=True)  31 us
    transpose x4, local copies, waits for them, and re-layouts, compose_blocks(): jnp.einsum('kab,kjbc->kjac', earlier_full[row_number], later_full, prefer...  21.6 us
    dot_general x4, matrix products, compose_blocks(): jnp.einsum('jk,kjac->jac', counts[row_number], products, precision=lax.Pr...  17.3 us
    dot_general x4, matrix products, compose_blocks(): jnp.einsum('kab,kjbc->kjac', earlier_full[row_number], later_full, prefer...  12 us
    all_to_all x1, starting transfers between devices, run_pools_in(): lax.all_to_all(jnp.stack([mine_x] * lax.axis_size('row')), 'row', 0, 0)  5.2 us
  transfers between devices with their start and end apart: 2, of which 1 were waited for; matrix products, arithmetic and copies ran while one was open for 1% of the time, Pallas kernels for 0%

profile of v1, /device:TPU:0, one launch (start us, length us, event | category | flops | bytes accessed | tf_op | source)
XLA Modules:
  0.0 106.7 jit_solution(12155650640816232257)
XLA Ops:
  6.5 0.7 convert_bitcast_fusion
  7.2 1.0 multiply_bitcast_fusion
  8.3 1.8 %stack.12 = bf16[8,1,8,128,128]{4,3,2,1,0:T(8,128)(2,1)} broadcast(bf16[8,128,128]{2,1,0:T(8,128)(2,1)S(1)} %multiply_bitcast_fusion), dimensions={2,3,4} | broadcast | bytes 2359296 | tf_op jit(solution)/shard_map/stack | solution.py:34
  10.1 5.2 %all-to-all-start = ((bf16[8,1,8,128,128]{4,3,2,1,0:T(8,128)(2,1)}), bf16[8,1,8,128,128]{4,3,2,1,0:T(8,128)(2,1)S(1)}, u32[]{:S(2)}, u32[]{:S(2)}) async-start(bf16[8,1,8,128,128]{4,3,2,1,0:T(8,128)(2,1)} %stack.12), calls=%async_computation | async-start | bytes 4194304 | tf_op jit(solution)/shard_map/all_to_all | solution.py:34
  15.3 0.0 all-gather.2.cloned.1.call-start
  15.4 0.1 copy.7
  15.5 0.8 broadcast_multiply_fusion
  16.3 0.0 all-gather.2.cloned.1.call-update
  16.3 0.1 convert_reduce_fusion
  16.4 31.0 %all-gather.2.cloned.1.call-done = bf16[4,8,128,128]{3,2,1,0:T(8,128)(2,1)} async-done(((bf16[4,2,128,128]{3,2,1,0:T(8,128)(2,1)}), bf16[4,8,128,128]{3,2,1,0:T(8,128)(2,1)}) %all-gather.2.cloned.1.call-update) | async-done | bytes 1048592 | tf_op jit(solution)/shard_map/all_gather | solution.py:38
  47.4 0.0 all-to-all-done
  47.4 3.7 %convolution_bitcast_fusion.2 = f32[8,8,128,128]{2,3,1,0:T(8,128)} fusion(bf16[8,1,8,128,128]{4,3,2,1,0:T(8,128)(2,1)S(1)} %all-to-all-done, bf16[4,8,128,128]{3,2,1,0:T(8,128)(2,1)} %all-gather.2.cloned.1.call-done), kind=kOutput, calls=%fused_computation.2 | convolution fusion | flops 268435456 | bytes 6553600 | tf_op jit(solution)/shard_map/kab,kjbc->kjac/dot_general | solution.py:16
  51.2 5.5 %copy.14 = f32[8,8,128,128]{3,0,2,1:T(8,128)} copy(f32[8,8,128,128]{2,3,1,0:T(8,128)} %convolution_bitcast_fusion.2) | data formatting | bytes 8388608 | tf_op jit(solution)/shard_map/kab,kjbc->kjac/transpose | solution.py:16
  56.6 2.8 %convolution_bitcast_fusion.1 = f32[8,8,128,128]{2,3,1,0:T(8,128)} fusion(bf16[8,1,8,128,128]{4,3,2,1,0:T(8,128)(2,1)S(1)} %all-to-all-done, bf16[4,8,128,128]{3,2,1,0:T(8,128)(2,1)S(1)} %copy-done.3), kind=kOutput, calls=%fused_computation.1 | convolution fusion | flops 268435456 | bytes 6553600 | tf_op jit(solution)/shard_map/kab,kjbc->kjac/dot_general | solution.py:16
  59.4 5.4 %copy.18 = f32[8,8,128,128]{3,0,2,1:T(8,128)} copy(f32[8,8,128,128]{2,3,1,0:T(8,128)} %convolution_bitcast_fusion.1) | data formatting | bytes 8388608 | tf_op jit(solution)/shard_map/kab,kjbc->kjac/transpose | solution.py:16
  64.8 2.7 %convolution_bitcast_fusion = f32[8,8,128,128]{2,3,1,0:T(8,128)} fusion(bf16[8,1,8,128,128]{4,3,2,1,0:T(8,128)(2,1)S(1)} %all-to-all-done, bf16[4,8,128,128]{3,2,1,0:T(8,128)(2,1)S(1)} %copy-done.3), kind=kOutput, calls=%fused_computation | convolution fusion | flops 268435456 | bytes 6553600 | tf_op jit(solution)/shard_map/kab,kjbc->kjac/dot_general | solution.py:16
  67.5 5.4 %copy.22 = f32[8,8,128,128]{3,0,2,1:T(8,128)} copy(f32[8,8,128,128]{2,3,1,0:T(8,128)} %convolution_bitcast_fusion) | data formatting | bytes 8388608 | tf_op jit(solution)/shard_map/kab,kjbc->kjac/transpose | solution.py:16
  72.9 2.8 %convolution_bitcast_fusion.3 = f32[8,8,128,128]{2,3,1,0:T(8,128)} fusion(bf16[8,1,8,128,128]{4,3,2,1,0:T(8,128)(2,1)S(1)} %all-to-all-done, bf16[4,8,128,128]{3,2,1,0:T(8,128)(2,1)S(1)} %copy-done.3), kind=kOutput, calls=%fused_computation.3 | convolution fusion | flops 268435456 | bytes 6553600 | tf_op jit(solution)/shard_map/kab,kjbc->kjac/dot_general | solution.py:16
  75.6 5.3 %copy.10 = f32[8,8,128,128]{3,0,2,1:T(8,128)} copy(f32[8,8,128,128]{2,3,1,0:T(8,128)} %convolution_bitcast_fusion.3) | data formatting | bytes 8388608 | tf_op jit(solution)/shard_map/kab,kjbc->kjac/transpose | solution.py:16
  81.0 6.1 %fusion.6 = f32[8,1,128,128]{3,1,2,0:T(1,128)S(1)} fusion(f32[8,8,1,1]{1,2,3,0:T(1,128)S(1)} %bitcast.92, f32[8,8,128,128]{3,0,2,1:T(8,128)} %copy.14), kind=kOutput, calls=%fused_computation.20 | convolution fusion | flops 12582912 | bytes 4718848 | tf_op jit(solution)/shard_map/jk,kjac->jac/dot_general | solution.py:23
  87.1 3.7 %fusion.7 = f32[8,1,128,128]{3,1,2,0:T(1,128)S(1)} fusion(f32[8,8,1,1]{1,2,3,0:T(1,128)S(1)} %bitcast.91, f32[8,8,128,128]{3,0,2,1:T(8,128)S(1)} %copy-done), kind=kOutput, calls=%fused_computation.21 | convolution fusion | flops 12582912 | bytes 4718848 | tf_op jit(solution)/shard_map/jk,kjac->jac/dot_general | solution.py:23
  90.9 3.7 %fusion.8 = f32[8,1,128,128]{3,1,2,0:T(1,128)S(1)} fusion(f32[8,8,1,1]{1,2,3,0:T(1,128)S(1)} %bitcast.90, f32[8,8,128,128]{3,0,2,1:T(8,128)S(1)} %copy-done.1), kind=kOutput, calls=%fused_computation.22 | convolution fusion | flops 12582912 | bytes 4718848 | tf_op jit(solution)/shard_map/jk,kjac->jac/dot_general | solution.py:23
  94.6 3.7 %fusion.5 = f32[8,1,128,128]{3,1,2,0:T(1,128)S(1)} fusion(f32[8,8,1,1]{1,2,3,0:T(1,128)S(1)} %bitcast.89, f32[8,8,128,128]{3,0,2,1:T(8,128)S(1)} %copy-done.2), kind=kOutput, calls=%fused_computation.19 | convolution fusion | flops 12582912 | bytes 4718848 | tf_op jit(solution)/shard_map/jk,kjac->jac/dot_general | solution.py:23
  98.4 1.5 %pad_maximum_fusion = f32[4,8,128,128]{3,2,1,0:T(8,128)} fusion(f32[1,8,128,128]{3,2,1,0:T(8,128)S(1)} %bitcast.87, f32[1,8,128,128]{3,2,1,0:T(8,128)S(1)} %bitcast.86, f32[1,8,128,128]{3,2,1,0:T(8,128)S(1)} %bitcast.85, f32[1,8,128,128]{3,2,1,0:T(8,128)S(1)} %bitcast.88), kind=kLoop, calls=%fused_computation.4 | loop fusion | flops 1572864 | bytes 4194304 | tf_op jit(solution)/shard_map/stack | solution.py:27
  (16 shorter events, 0.0 us)
Async XLA Ops:
  6.5 8.8 %copy-start.6 = (s32[4,2]{0,1:T(2,128)S(1)}, s32[4,2]{0,1:T(2,128)}, u32[]{:S(2)}) copy-start(s32[4,2]{0,1:T(2,128)} %param.7) | copy-start | bytes 100
  6.5 8.9 %copy-start.4 = (bf16[4,2,128,128]{3,2,1,0:T(8,128)(2,1)S(1)}, bf16[4,2,128,128]{3,2,1,0:T(8,128)(2,1)}, u32[]{:S(2)}) copy-start(bf16[4,2,128,128]{3,2,1,0:T(8,128)(2,1)} %param.5) | copy-start | bytes 786436
  6.5 9.8 %copy-start.5 = (s32[4,8,48]{2,1,0:T(8,128)S(1)}, s32[4,8,48]{2,1,0:T(8,128)}, u32[]{:S(2)}) copy-start(s32[4,8,48]{2,1,0:T(8,128)} %param.9) | copy-start | bytes 18436
  10.1 37.3 %all-to-all-start = ((bf16[8,1,8,128,128]{4,3,2,1,0:T(8,128)(2,1)}), bf16[8,1,8,128,128]{4,3,2,1,0:T(8,128)(2,1)S(1)}, u32[]{:S(2)}, u32[]{:S(2)}) async-start(bf16[8,1,8,128,128]{4,3,2,1,0:T(8,128)(2,1)} %stack.12), calls=%async_computation | async-start | bytes 4194304 | tf_op jit(solution)/shard_map/all_to_all | solution.py:34
  15.3 32.1 %all-gather.2.cloned.1.call-start = ((), (), s32[]{:S(2)}) async-start(), calls=%async_computation.1 | async-start | bytes 1310720 | tf_op jit(solution)/shard_map/all_gather | solution.py:38
  51.1 5.5 %copy-start.3 = (bf16[4,8,128,128]{3,2,1,0:T(8,128)(2,1)S(1)}, bf16[4,8,128,128]{3,2,1,0:T(8,128)(2,1)}, u32[]{:S(2)}) copy-start(bf16[4,8,128,128]{3,2,1,0:T(8,128)(2,1)} %all-gather.2.cloned.1.call-done) | copy-start | bytes 3145732
  81.0 6.1 %copy-start = (f32[8,8,128,128]{3,0,2,1:T(8,128)S(1)}, f32[8,8,128,128]{3,0,2,1:T(8,128)}, u32[]{:S(2)}) copy-start(f32[8,8,128,128]{3,0,2,1:T(8,128)} %copy.18) | copy-start | bytes 12582916
  81.0 9.9 %copy-start.1 = (f32[8,8,128,128]{3,0,2,1:T(8,128)S(1)}, f32[8,8,128,128]{3,0,2,1:T(8,128)}, u32[]{:S(2)}) copy-start(f32[8,8,128,128]{3,0,2,1:T(8,128)} %copy.22) | copy-start | bytes 12582916
  87.1 7.5 %copy-start.2 = (f32[8,8,128,128]{3,0,2,1:T(8,128)S(1)}, f32[8,8,128,128]{3,0,2,1:T(8,128)}, u32[]{:S(2)}) copy-start(f32[8,8,128,128]{3,0,2,1:T(8,128)} %copy.10) | copy-start | bytes 12582916
Sparse Core Ops, SparseCore 0:
  17.7 29.6 all-gather.1
